TPU v7x, 32 devices: a whole 2x2x4 slice. The times are simulated.
32 devices in a mesh: seq: 8 (over y, x, core), dp: 4 (over z).
Axes of the slice: x: 2, y: 2, z: 4, core: 2. Of those that a mesh axis runs over, the one named last changes fastest.
Arguments:
- history: bfloat16 [9, 1024, 4096], P(None, 'seq', 'dp'), may hold values from -6 to 6
- cotangent: bfloat16 [1024, 4096], P('seq', 'dp'), may hold values from -6 to 6
- bucket_len: int32 [4, 8, 2], P('dp', 'seq'), may hold values from 32 to 96, as said below
- valid_len: int32 [4, 8, 2], P('dp', 'seq'), may hold values from 1 to 96, as said below
- gen_gain: float32 [1024], replicated, may hold values from 0.25 to 1.75
- gen_in: bfloat16 [1024, 40], replicated, may hold values from -0.1875 to 0.1875
- gen_out: float32 [40, 4, 9], replicated, may hold values from -1 to 1
- gen_bias: float32 [4, 9], replicated, may hold values from -3 to 3
- norm_gain: float32 [2, 1024], replicated, may hold values from 0.25 to 1.75
- norm_bias: float32 [2, 1024], replicated, may hold values from -2 to 2
- w_in: bfloat16 [1024, 7, 1024], P('seq'), may hold values from -0.1875 to 0.1875
- in_bias: float32 [7, 1024], replicated, may hold values from -2 to 2
- w_out: bfloat16 [1024, 1024], P('seq'), may hold values from -0.75 to 0.75
- w_down: bfloat16 [1024, 4096], P('seq'), may hold values from -0.09375 to 0.09375
- out_bias: float32 [1024], replicated, may hold values from -2 to 2
Outputs:
- new_state: bfloat16 [1024, 4096], P('seq', 'dp')
- history_grad: bfloat16 [9, 1024, 4096], P(None, 'seq', 'dp')
- mix_mean: float32 [4, 9], replicated
- mix_var: float32 [4, 9], replicated
- gen_gain_grad: float32 [1024], replicated
- gen_in_grad: float32 [1024, 40], replicated
- gen_out_grad: float32 [40, 4, 9], replicated
- gen_bias_grad: float32 [4, 9], replicated
- norm_gain_grad: float32 [2, 1024], replicated
- norm_bias_grad: float32 [2, 1024], replicated
- w_in_grad: float32 [1024, 7, 1024], P('seq')
- in_bias_grad: float32 [7, 1024], replicated
- w_out_grad: float32 [1024, 1024], P('seq')
- w_down_grad: float32 [1024, 4096], P('seq')
- out_bias_grad: float32 [1024], replicated
Inputs may be any that keep to these rules, and one draw needn't show every extreme that they name: `bucket_len`: the two buckets of one token block together hold 128 tokens. Each bucket's valid tokens are its first valid_len tokens, at least one and at most the bucket's length.
All inputs are finite; a program needn't handle non-finite values.
Results may differ from a plain program's by a relative error of at most 0.015.
Values may be sent and summed in bfloat16 or wider, within the bound.
A program may use at most 256 MiB of HBM per device.

v0:
```python
import math
import jax
import jax.numpy as jnp
from jax import lax
from jax.sharding import PartitionSpec as P

HEADS = 16
HEAD_DIM = 64
ROT = 16
ln_eps = 1e-05
rms_eps = 1e-06
masked_score = -1e30
highest = lax.Precision.HIGHEST


def gelu_exact(values):
    return jax.nn.gelu(values, approximate=False)


def rotary_tables(position):
    freq_index = jnp.arange(ROT // 2, dtype=jnp.float32)
    inverse_freq = jnp.exp(freq_index * (-2.0 * math.log(10000.0) / ROT))
    angles = position.astype(jnp.float32)[:, None] * inverse_freq[None, :]
    return (jnp.cos(angles), jnp.sin(angles))


def rotate(values, cosine, sine):
    half = ROT // 2
    former = values[..., :half]
    latter = values[..., half:ROT]
    cos_heads = cosine[:, None, :]
    sin_heads = sine[:, None, :]
    return jnp.concatenate(
        [
            former * cos_heads - latter * sin_heads,
            latter * cos_heads + former * sin_heads,
            values[..., ROT:],
        ],
        axis=-1,
    )


def token_layout(lengths, counts, tokens):
    index = jnp.arange(tokens, dtype=jnp.int32)
    second = index >= lengths[0]
    position = index - jnp.where(second, lengths[0], 0)
    valid = position < jnp.where(second, counts[1], counts[0])
    return (second, position, valid)


def normalize(streams):
    centre = jnp.mean(streams, axis=-1, keepdims=True)
    centred = streams - centre
    inverse = lax.rsqrt(jnp.mean(centred * centred, axis=-1, keepdims=True) + ln_eps)
    return (centred * inverse, inverse)


def normalize_back(grad_scaled, scaled, inverse):
    mean_grad = jnp.mean(grad_scaled, axis=-1, keepdims=True)
    mean_along = jnp.mean(grad_scaled * scaled, axis=-1, keepdims=True)
    return inverse * (grad_scaled - mean_grad - scaled * mean_along)


def per_device(
    history,
    cotangent,
    bucket_len,
    valid_len,
    gen_gain,
    gen_in,
    gen_out,
    gen_bias,
    norm_gain,
    norm_bias,
    w_in,
    in_bias,
    w_out,
    w_down,
    out_bias,
):
    states = history.shape[0]
    stacked = jnp.concatenate([history, cotangent[None]], axis=0)
    arrived = lax.all_to_all(stacked, "seq", split_axis=2, concat_axis=1, tiled=True)
    arrived_rows = jnp.swapaxes(arrived, 1, 2)
    hist_local = arrived_rows[:states]
    cot_local = arrived_rows[states]
    tokens = hist_local.shape[1]
    width = hist_local.shape[2]
    second, position, valid = token_layout(bucket_len.reshape(2), valid_len.reshape(2), tokens)
    valid_float = valid.astype(jnp.float32)
    last = hist_local[states - 1].astype(jnp.float32)
    rms = lax.rsqrt(jnp.mean(last * last, axis=-1, keepdims=True) + rms_eps)
    gen_normed = (last * rms * gen_gain).astype(jnp.bfloat16)
    gen_pre = jnp.dot(gen_normed, gen_in, preferred_element_type=jnp.float32)
    gen_hidden, gen_pull = jax.vjp(gelu_exact, gen_pre)
    mixing = jnp.einsum("th,hsj->tsj", gen_hidden, gen_out, precision=highest) + gen_bias
    weighted = mixing * valid_float[:, None, None]
    stat_sums = jnp.sum(weighted, axis=0)
    stat_squares = jnp.sum(weighted * mixing, axis=0)
    stat_count = jnp.sum(valid_float)
    streams = mixing[:, :, 0].T[:, :, None] * hist_local[0]
    for state in range(1, states):
        streams = streams + mixing[:, :, state].T[:, :, None] * hist_local[state]
    scaled, inverse = normalize(streams)
    normed_attn = (scaled[:3] * norm_gain[0] + norm_bias[0]).astype(jnp.bfloat16)
    normed_mlp = (scaled[3] * norm_gain[1] + norm_bias[1]).astype(jnp.bfloat16)
    piece = lax.all_gather(w_in, "seq", axis=0, tiled=True)
    attn_part = jnp.einsum(
        "stk,nsk->stn", normed_attn, piece[:, :3], preferred_element_type=jnp.float32
    )
    mlp_part = jnp.einsum(
        "tk,njk->jtn", normed_mlp, piece[:, 3:], preferred_element_type=jnp.float32
    )
    projected = jnp.concatenate([attn_part, mlp_part], axis=0) + in_bias[:, None, :]
    cosine, sine = rotary_tables(position)
    heads_shape = (tokens, HEADS, HEAD_DIM)
    queries = (rotate(projected[0].reshape(heads_shape), cosine, sine) * HEAD_DIM ** (-0.5)).astype(
        jnp.bfloat16
    )
    keys = rotate(projected[1].reshape(heads_shape), cosine, sine).astype(jnp.bfloat16)
    values = projected[2].reshape(heads_shape).astype(jnp.bfloat16)
    index = jnp.arange(tokens, dtype=jnp.int32)
    allowed = (
        (second[:, None] == second[None, :]) & (index[None, :] <= index[:, None]) & valid[None, :]
    )
    scores = jnp.einsum("qhd,khd->hqk", queries, keys, preferred_element_type=jnp.float32)
    scores = jnp.where(allowed[None], scores, masked_score)
    top = jnp.max(scores, axis=-1, keepdims=True)
    weights = jnp.exp(scores - top)
    weight_total = jnp.sum(weights, axis=-1, keepdims=True)
    log_total = top + jnp.log(weight_total)
    probs_low = (weights / weight_total).astype(jnp.bfloat16)
    attended = jnp.einsum("hqk,khd->qhd", probs_low, values, preferred_element_type=jnp.float32)
    attn_low = attended.reshape(tokens, width).astype(jnp.bfloat16)
    gelu_up, up_pull = jax.vjp(gelu_exact, projected[3:])
    gelu_low = gelu_up.astype(jnp.bfloat16)
    grad_out_low = jnp.where(valid[:, None], cot_local, jnp.zeros_like(cot_local))
    piece_out, piece_down = lax.all_gather((w_out, w_down), "seq", axis=0, tiled=True)
    down_part = piece_down.reshape(piece_down.shape[0], 4, width)
    result = jnp.einsum("tk,nk->tn", attn_low, piece_out, preferred_element_type=jnp.float32)
    branch = result + jnp.einsum(
        "jtk,njk->tn", gelu_low, down_part, preferred_element_type=jnp.float32
    )
    new_local = (streams[3] + branch + out_bias).astype(jnp.bfloat16)
    piece_out = lax.all_gather(w_out, "seq", axis=0, tiled=True)
    piece_down = lax.all_gather(w_down, "seq", axis=0, tiled=True)
    count = piece_out.shape[0]
    part = grad_out_low
    attn_add = jnp.einsum("tn,nk->tk", part, piece_out, preferred_element_type=jnp.float32)
    gelu_add = jnp.einsum(
        "tn,njk->jtk", part, piece_down.reshape(count, 4, width), preferred_element_type=jnp.float32
    )
    grad_attn = attn_add
    part = grad_out_low
    term_out = jnp.einsum("tn,tk->nk", part, attn_low, preferred_element_type=jnp.float32)
    term_down = jnp.einsum(
        "tn,jtk->njk", part, gelu_low, preferred_element_type=jnp.float32
    ).reshape(lax.axis_size("seq") * w_out.shape[0], 4 * width)
    out_grads = lax.psum_scatter(
        jnp.concatenate([term_out, term_down], axis=1).astype(jnp.bfloat16),
        "seq",
        scatter_dimension=0,
        tiled=True,
    )
    out_bias_grad = jnp.sum(grad_out_low.astype(jnp.float32), axis=0)
    grad_attended = grad_attn.astype(jnp.bfloat16).reshape(heads_shape)
    rescored = jnp.einsum("qhd,khd->hqk", queries, keys, preferred_element_type=jnp.float32)
    probs = jnp.where(allowed[None], jnp.exp(rescored - log_total), 0.0)
    grad_values = jnp.einsum(
        "hqk,qhd->khd",
        probs.astype(jnp.bfloat16),
        grad_attended,
        preferred_element_type=jnp.float32,
    )
    grad_probs = jnp.einsum(
        "qhd,khd->hqk", grad_attended, values, preferred_element_type=jnp.float32
    )
    grad_scores = (
        probs * (grad_probs - jnp.sum(probs * grad_probs, axis=-1, keepdims=True))
    ).astype(jnp.bfloat16)
    grad_queries = jnp.einsum(
        "hqk,khd->qhd", grad_scores, keys, preferred_element_type=jnp.float32
    ) * HEAD_DIM ** (-0.5)
    grad_keys = jnp.einsum("hqk,qhd->khd", grad_scores, queries, preferred_element_type=jnp.float32)
    grad_up = up_pull(gelu_add)[0]
    grad_proj = jnp.concatenate(
        [
            rotate(grad_queries, cosine, -sine).reshape(1, tokens, width),
            rotate(grad_keys, cosine, -sine).reshape(1, tokens, width),
            grad_values.reshape(1, tokens, width),
            grad_up,
        ],
        axis=0,
    )
    in_bias_grad = jnp.sum(grad_proj, axis=1)
    grad_proj_low = grad_proj.astype(jnp.bfloat16)
    piece = lax.all_gather(w_in, "seq", axis=0, tiled=True)
    part = grad_proj_low
    attn_add = jnp.einsum(
        "stn,nsk->stk", part[:3], piece[:, :3], preferred_element_type=jnp.float32
    )
    mlp_add = jnp.einsum("jtn,njk->tk", part[3:], piece[:, 3:], preferred_element_type=jnp.float32)
    part = grad_proj_low
    attn_term = jnp.einsum(
        "stn,stk->nsk", part[:3], normed_attn, preferred_element_type=jnp.float32
    )
    mlp_term = jnp.einsum("jtn,tk->njk", part[3:], normed_mlp, preferred_element_type=jnp.float32)
    in_grads = lax.psum_scatter(
        jnp.concatenate([attn_term, mlp_term], axis=1).astype(jnp.bfloat16),
        "seq",
        scatter_dimension=0,
        tiled=True,
    )
    norm_gain_grad = jnp.stack(
        [jnp.sum(attn_add * scaled[:3], axis=(0, 1)), jnp.sum(mlp_add * scaled[3], axis=0)]
    )
    norm_bias_grad = jnp.stack([jnp.sum(attn_add, axis=(0, 1)), jnp.sum(mlp_add, axis=0)])
    grad_attn_streams = normalize_back(attn_add * norm_gain[0], scaled[:3], inverse[:3])
    grad_mlp_stream = normalize_back(
        mlp_add * norm_gain[1], scaled[3], inverse[3]
    ) + grad_out_low.astype(jnp.float32)
    grad_streams = jnp.concatenate([grad_attn_streams, grad_mlp_stream[None]], axis=0)
    grad_mixing = jnp.stack(
        [
            jnp.einsum(
                "std,td->ts", grad_streams, hist_local[state].astype(jnp.float32), precision=highest
            )
            for state in range(states)
        ],
        axis=-1,
    )
    hist_terms = [
        jnp.einsum("ts,std->td", mixing[:, :, state], grad_streams, precision=highest)
        for state in range(states)
    ]
    gen_bias_grad = jnp.sum(grad_mixing, axis=0)
    gen_out_grad = jnp.einsum("th,tsj->hsj", gen_hidden, grad_mixing, precision=highest)
    grad_hidden = jnp.einsum("tsj,hsj->th", grad_mixing, gen_out, precision=highest)
    grad_pre_low = gen_pull(grad_hidden)[0].astype(jnp.bfloat16)
    gen_in_grad = jnp.einsum(
        "tk,th->kh", gen_normed, grad_pre_low, preferred_element_type=jnp.float32
    )
    grad_gen = jnp.einsum("th,kh->tk", grad_pre_low, gen_in, preferred_element_type=jnp.float32)
    gen_gain_grad = jnp.sum(grad_gen * last * rms, axis=0)
    gained = grad_gen * gen_gain
    grad_last = rms * gained - last * (rms * rms * rms) * jnp.mean(
        gained * last, axis=-1, keepdims=True
    )
    hist_stack = jnp.stack(hist_terms[: states - 1] + [hist_terms[states - 1] + grad_last]).astype(
        jnp.bfloat16
    )
    departing = jnp.swapaxes(jnp.concatenate([new_local[None], hist_stack], axis=0), 1, 2)
    returned = lax.all_to_all(departing, "seq", split_axis=1, concat_axis=2, tiled=True)
    w_in_grad, out_total = (
        lax.psum(in_grads, "dp").astype(jnp.float32),
        lax.psum(out_grads, "dp").astype(jnp.float32),
    )
    w_out_grad = out_total[:, :width]
    w_down_grad = out_total[:, width:]
    joined = lax.psum(
        (
            gen_gain_grad,
            gen_in_grad,
            gen_out_grad,
            gen_bias_grad,
            norm_gain_grad,
            norm_bias_grad,
            in_bias_grad,
            out_bias_grad,
            stat_sums,
            stat_squares,
            stat_count,
        ),
        ("seq", "dp"),
    )
    small_totals = joined[:8]
    stat_totals = joined[8:]
    mix_mean = stat_totals[0] / stat_totals[2]
    mix_var = stat_totals[1] / stat_totals[2] - mix_mean * mix_mean
    return (
        returned[0],
        returned[1:],
        mix_mean,
        mix_var,
        small_totals[0],
        small_totals[1],
        small_totals[2],
        small_totals[3],
        small_totals[4],
        small_totals[5],
        w_in_grad,
        small_totals[6],
        w_out_grad,
        w_down_grad,
        small_totals[7],
    )


def solution(mesh):
    in_specs = (
        P(None, "seq", "dp"),
        P("seq", "dp"),
        P("dp", "seq", None),
        P("dp", "seq", None),
        P(),
        P(),
        P(),
        P(),
        P(),
        P(),
        P("seq", None, None),
        P(),
        P("seq", None),
        P("seq", None),
        P(),
    )
    out_specs = (
        P("seq", "dp"),
        P(None, "seq", "dp"),
        P(),
        P(),
        P(),
        P(),
        P(),
        P(),
        P(),
        P(),
        P("seq", None, None),
        P(),
        P("seq", None),
        P("seq", None),
        P(),
    )
    return jax.shard_map(
        per_device, mesh=mesh, in_specs=in_specs, out_specs=out_specs, check_vma=False
    )
```

profile of v0, /device:TPU:8, one launch (start us, length us, event | category | flops | bytes accessed | tf_op | source)
XLA Modules:
  0.0 705.1 jit_solution(17909491425658481265)
XLA Ops:
  11.4 7.4 %copy.110 = bf16[9,128,1024]{1,0,2:T(8,128)(2,1)} copy(bf16[9,128,1024]{2,1,0:T(8,128)(2,1)S(1)} %copy-done.17) | data formatting | bytes 4718592 | tf_op args[0]
  18.8 6.1 pad_maximum_fusion.2
  24.9 4.7 all-to-all-start
  33.1 64.4 %all-to-all-done = bf16[10,128,1024]{1,0,2:T(8,128)(2,1)} async-done(((bf16[10,128,1024]{1,0,2:T(8,128)(2,1)}), bf16[10,128,1024]{1,0,2:T(8,128)(2,1)}, u32[]{:S(2)}, u32[]{:S(2)}) %all-to-all-start) | async-done | bytes 2621472 | tf_op jit(solution)/shard_map/all_to_all | solution.py:83
  97.5 5.4 copy.298
  117.8 33.5 %all-gather.4.cloned.1.call-done = bf16[1024,7,1024]{2,0,1:T(8,128)(2,1)} async-done(((bf16[128,7,1024]{2,0,1:T(8,128)(2,1)}), bf16[1024,7,1024]{2,0,1:T(8,128)(2,1)}) %all-gather.4.cloned.1.call-update) | async-done | bytes 14680080 | tf_op jit(solution)/shard_map/all_gather | solution.py:107
  151.3 5.0 fusion.6
  156.3 6.3 fusion.22
  184.9 7.3 %multiply_convert_fusion = (bf16[4,128,1024]{2,1,0:T(8,128)(2,1)}, f32[4,128,1024]{2,1,0:T(8,128)}) fusion(f32[7,128,1024]{2,1,0:T(8,128)} %copy-done.3), kind=kLoop, calls=%fused_computation.30 | loop fusion | flops 34078720 | bytes 5242880 | tf_op jit(solution)/shard_map/convert_element_type | solution.py:136
  192.2 16.9 %all-gather.8.cloned.1.call-done = bf16[1024,4096]{0,1:T(8,128)(2,1)} async-done(((bf16[128,4096]{0,1:T(8,128)(2,1)}), bf16[1024,4096]{0,1:T(8,128)(2,1)}) %all-gather.8.cloned.1.call-update) | async-done | bytes 8388624 | tf_op jit(solution)/shard_map/all_gather | solution.py:138
  209.1 8.0 %fusion.15 = f32[4,128,1024]{2,1,0:T(8,128)S(1)} fusion(f32[4,128,1024]{2,1,0:T(8,128)} %get-tuple-element.106, f32[7,128,1024]{2,1,0:T(8,128)} %copy-done.3, bf16[1024,4,1024]{0,2,1:T(8,128)(2,1)} %bitcast.374, pred[128]{0:T(512)(128)(4,1)S(1)} %copy-done.57, bf16[10,128,1024]{2,1,0:T(8,128)(2,1)} %bitcast.365), kind=kOutput, calls=%fused_computation.28 | convolution fusion | flops 1080688640 | bytes 14942336 | tf_op jit(solution)/shard_map/tn,njk->jtk/dot_general | solution.py:150
  223.3 8.3 %pad_maximum_fusion = bf16[1024,7,1024]{0,2,1:T(8,128)(2,1)} fusion(bf16[1024,4,1024]{0,2,1:T(8,128)(2,1)S(1)} %convert_bitcast_fusion, bf16[1024,3,1024]{0,2,1:T(8,128)(2,1)S(1)} %convert_bitcast_fusion.1), kind=kLoop, calls=%fused_computation | loop fusion | flops 7340032 | bytes 29360128 | tf_op jit(solution)/shard_map/concatenate | solution.py:209
  231.6 18.5 %copy.186 = bf16[1024,7168]{1,0:T(8,128)(2,1)} copy(bf16[1024,7168]{0,1:T(8,128)(2,1)} %bitcast.360) | data formatting | bytes 29360128
  264.6 6.3 pad_maximum_fusion.1
  278.1 5.9 multiply_reduce_fusion.5
  284.0 5.0 multiply_reduce_fusion.1
  291.5 4.8 fusion.68
  296.3 4.8 fusion.66
  301.2 5.0 fusion.64
  306.3 4.8 fusion.62
  311.8 4.8 fusion.60
  317.2 5.2 fusion.58
  323.1 4.8 fusion.56
  328.5 4.8 fusion.54
  333.9 5.6 fusion.52
  343.5 5.2 fusion.154
  348.8 4.9 convolution_bitcast_fusion.1
  388.6 51.7 %reduce-scatter.5.cloned.1.call-done = bf16[128,5120]{1,0:T(8,128)(2,1)} async-done(((bf16[1024,5120]{1,0:T(8,128)(2,1)}), bf16[128,5120]{1,0:T(8,128)(2,1)}) %reduce-scatter.5.cloned.1.call-update) | async-done | bytes 1310736 | tf_op jit(solution)/shard_map/reduce_scatter | solution.py:159
  457.2 6.8 copy.129
  464.1 4.8 all-to-all-start.1
  472.8 81.4 %all-reduce = (f32[4,9]{1,0:T(4,128)S(1)}, f32[]{:T(128)}, f32[4,9]{1,0:T(4,128)S(1)}, f32[1024]{0:T(1024)}, f32[40,4,9]{0,2,1:T(8,128)S(1)}, /*index=5*/f32[4,9...) all-reduce(f32[4,9]{1,0:T(4,128)S(1)} %copy-done.85, ...), channel_id=1, replica_groups=mesh['seq'=8,'dp'=4] {'seq','dp'}, use_global_device_ids=true, to_apply=%region_12.13 | all-reduce | flops 14861 | bytes 118888 | tf_op jit(solution)/shard_map/psum | solution.py:260
  574.8 121.5 %all-reduce.5.cloned.1.call-done = f32[1024,40]{0,1:T(8,128)} async-done(((f32[1024,40]{0,1:T(8,128)}), f32[1024,40]{0,1:T(8,128)}) %all-reduce.5.cloned.1.call-update) | async-done | bytes 163856 | tf_op jit(solution)/shard_map/psum | solution.py:260
  (345 shorter events, 159.7 us)
Async XLA Ops:
  7.2 101.2 %copy-start = (bf16[1024,40]{0,1:T(8,128)(2,1)S(1)}, bf16[1024,40]{0,1:T(8,128)(2,1)}, u32[]{:S(2)}) copy-start(bf16[1024,40]{0,1:T(8,128)(2,1)} %param.20) | copy-start | bytes 245764
  7.2 108.2 %all-gather.6.cloned.1.call-start = ((), (), s32[]{:S(2)}) async-start(), calls=%async_computation.5 | async-start | bytes 2359296 | tf_op jit(solution)/shard_map/all_gather | solution.py:138
  7.9 143.4 %all-gather.4.cloned.1.call-start = ((), (), s32[]{:S(2)}) async-start(), calls=%async_computation.4 | async-start | bytes 16515072 | tf_op jit(solution)/shard_map/all_gather | solution.py:107
  8.7 200.4 %all-gather.8.cloned.1.call-start = ((), (), s32[]{:S(2)}) async-start(), calls=%async_computation.6 | async-start | bytes 9437184 | tf_op jit(solution)/shard_map/all_gather | solution.py:138
  24.9 8.1 %copy-start.86 = (f32[2,1024]{1,0:T(2,128)S(1)}, f32[2,1024]{1,0:T(2,128)}, u32[]{:S(2)}) copy-start(f32[2,1024]{1,0:T(2,128)} %param.24) | copy-start | bytes 24580
  24.9 8.1 %copy-start.87 = (f32[2,1024]{1,0:T(2,128)S(1)}, f32[2,1024]{1,0:T(2,128)}, u32[]{:S(2)}) copy-start(f32[2,1024]{1,0:T(2,128)} %param.23) | copy-start | bytes 24580
  24.9 72.6 %all-to-all-start = ((bf16[10,128,1024]{1,0,2:T(8,128)(2,1)}), bf16[10,128,1024]{1,0,2:T(8,128)(2,1)}, u32[]{:S(2)}, u32[]{:S(2)}) async-start(bf16[10,128,1024]{1,0,2:T(8,128)(2,1)} %pad_maximum_fusion.2), calls=%async_computation | async-start | bytes 8388608 | tf_op jit(solution)/shard_map/all_to_all | solution.py:83
  29.6 355.1 %reduce-scatter.7.cloned.1.call-start = ((), (), s32[]{:S(2)}) async-start(), calls=%async_computation.9 | async-start | bytes 16515072
  32.2 83.3 %copy-start.56 = (pred[128]{0:T(512)(128)(4,1)}, pred[128]{0:T(512)(128)(4,1)S(1)}, u32[]{:S(2)}) copy-start(pred[128]{0:T(512)(128)(4,1)S(1)} %get-tuple-element.104) | copy-start | bytes 388
  33.0 118.3 %copy-start.78 = (f32[1,1024]{1,0:T(1,128)}, f32[1,1024]{1,0:T(1,128)S(1)}, u32[]{:S(2)}) copy-start(f32[1,1024]{1,0:T(1,128)S(1)} %get-tuple-element.152) | copy-start | bytes 12292
  33.0 123.3 %copy-start.82 = (f32[1,1024]{1,0:T(1,128)}, f32[1,1024]{1,0:T(1,128)S(1)}, u32[]{:S(2)}) copy-start(f32[1,1024]{1,0:T(1,128)S(1)} %get-tuple-element.153) | copy-start | bytes 12292
  156.3 6.3 copy-start.53
  184.9 24.2 %copy-start.57 = (pred[128]{0:T(512)(128)(4,1)S(1)}, pred[128]{0:T(512)(128)(4,1)}, u32[]{:S(2)}) copy-start(pred[128]{0:T(512)(128)(4,1)} %copy-done.56) | copy-start | bytes 388
  209.1 9.3 %copy-start.11 = (f32[1,128,1024]{2,1,0:T(8,128)S(1)}, f32[1,128,1024]{2,1,0:T(8,128)}, u32[]{:S(2)}) copy-start(f32[1,128,1024]{2,1,0:T(8,128)} %copy.127) | copy-start | bytes 1572868
  209.1 9.3 %copy-start.13 = (f32[1,128,1024]{2,1,0:T(8,128)S(1)}, f32[1,128,1024]{2,1,0:T(8,128)}, u32[]{:S(2)}) copy-start(f32[1,128,1024]{2,1,0:T(8,128)} %copy.126) | copy-start | bytes 1572868
  209.1 9.3 %copy-start.15 = (f32[1,128,1024]{2,1,0:T(8,128)S(1)}, f32[1,128,1024]{2,1,0:T(8,128)}, u32[]{:S(2)}) copy-start(f32[1,128,1024]{2,1,0:T(8,128)} %copy.125) | copy-start | bytes 1572868
  250.1 190.1 %reduce-scatter.5.cloned.1.call-start = ((), (), s32[]{:S(2)}) async-start(), calls=%async_computation.8 | async-start | bytes 11796480 | tf_op jit(solution)/shard_map/reduce_scatter | solution.py:159
  270.9 6.5 copy-start.61
  270.9 7.2 %copy-start.59 = (f32[4,128]{1,0:T(4,128)S(1)}, f32[4,128]{1,0:T(4,128)}, u32[]{:S(2)}) copy-start(f32[4,128]{1,0:T(4,128)} %copy-done.58) | copy-start | bytes 6148
  270.9 296.3 %all-reduce.7.cloned.1.call-start = ((), (), s32[]{:S(2)}) async-start(), calls=%async_computation.10 | async-start | bytes 6291456 | tf_op jit(solution)/shard_map/psum | solution.py:255
  339.5 9.3 %copy-start.4 = (bf16[4,128,1024]{2,1,0:T(8,128)(2,1)S(1)}, bf16[4,128,1024]{2,1,0:T(8,128)(2,1)}, u32[]{:S(2)}) copy-start(bf16[4,128,1024]{2,1,0:T(8,128)(2,1)} %get-tuple-element.105) | copy-start | bytes 3145732
  372.0 6.2 copy-start.39
  388.6 51.7 %copy-start.38 = (f32[128,4,1]{1,2,0:T(1,128)S(1)}, f32[128,4,1]{1,2,0:T(1,128)}, u32[]{:S(2)}) copy-start(f32[128,4,1]{1,2,0:T(1,128)} %copy.157) | copy-start | bytes 6148
  464.1 7.0 copy-start.91
  464.1 7.0 copy-start.93
  464.1 7.0 copy-start.90
  464.1 7.0 copy-start.92
  464.1 7.0 copy-start.7
  464.1 7.0 copy-start.12
  464.1 7.0 copy-start.14
  464.1 91.9 %all-to-all-start.1 = ((bf16[10,1024,128]{2,0,1:T(8,128)(2,1)}), bf16[10,1024,128]{2,0,1:T(8,128)(2,1)}, u32[]{:S(2)}, u32[]{:S(2)}) async-start(bf16[10,1024,128]{2,0,1:T(8,128)(2,1)} %copy.129), calls=%async_computation.1 | async-start | bytes 8388608 | tf_op jit(solution)/shard_map/all_to_all | solution.py:253
  469.0 227.3 %all-reduce.5.cloned.1.call-start = ((), (), s32[]{:S(2)}) async-start(), calls=%async_computation.7 | async-start | bytes 327680 | tf_op jit(solution)/shard_map/psum | solution.py:260
  (78 other events, 256.0 us)
Sparse Core Ops, SparseCore 0:
  9.9 33.7 all-gather.5
  45.6 105.6 all-gather.3
  153.2 55.8 all-gather.7
  250.2 104.6 reduce-scatter.6
  358.2 81.9 reduce-scatter.4
  442.5 120.2 all-reduce.6
  568.9 127.3 all-reduce.4
where the time goes:
time: 712 us; the launch traced here: 705 us
  waiting for transfers between devices  289 us (41%)
  matrix products  148 us (21%)
  local copies, waits for them, and re-layouts  115 us (16%)
  blocking collectives  81.4 us (11%)
  other arithmetic  46.1 us (6%)
  between operations  15.9 us (2%)
  starting transfers between devices  9.98 us (1%)
    psum x1, waiting for transfers between devices, per_device(): lax.psum((gen_gain_grad, gen_in_grad, gen_out_grad, gen_bias_grad, norm_g...  121 us
    psum x1, blocking collectives, per_device(): lax.psum((gen_gain_grad, gen_in_grad, gen_out_grad, gen_bias_grad, norm_g...  81.4 us
    all_to_all x1, waiting for transfers between devices, per_device(): lax.all_to_all(stacked, 'seq', split_axis=2, concat_axis=1, tiled=True)  64.4 us
    reduce_scatter x1, waiting for transfers between devices, per_device(): lax.psum_scatter(jnp.concatenate([term_out, term_down], axis=1).astype(jn...  51.7 us
    unnamed x218, local copies, waits for them, and re-layouts  50.6 us
    dot_general x9, matrix products, per_device(): jnp.einsum('std,td->ts', grad_streams, hist_local[state].astype(jnp.float...  44.5 us
    dot_general x9, matrix products, per_device(): jnp.einsum('ts,std->td', mixing[:, :, state], grad_streams, precision=hig...  40.6 us
    all_gather x1, waiting for transfers between devices, per_device(): piece = lax.all_gather(w_in, 'seq', axis=0, tiled=True)  33.5 us
  transfers between devices with their start and end apart: 9, of which 5 were waited for; matrix products, arithmetic and copies ran while one was open for 36% of the time, Pallas kernels for 0%

commit v1 on v0

--- a/solution.py
+++ b/solution.py
@@ -11,6 +11,22 @@
 rms_eps = 1e-06
 masked_score = -1e30
 highest = lax.Precision.HIGHEST
+
+
+def swapped_with_each(array, axis, split, join):
+    ways, here = (lax.axis_size(axis), lax.axis_index(axis))
+    width = array.shape[split] // ways
+    dims = list(array.shape)
+    dims[split] = width
+    height = dims[join]
+    dims[join] = height * ways
+    full = jnp.zeros(dims, array.dtype)
+    for mask in range(ways):
+        part = lax.dynamic_slice_in_dim(array, (here ^ mask) * width, width, axis=split)
+        if mask:
+            part = lax.ppermute(part, axis, [(d, d ^ mask) for d in range(ways)])
+        full = lax.dynamic_update_slice_in_dim(full, part, (here ^ mask) * height, axis=join)
+    return full
 
 
 def gelu_exact(values):
@@ -80,7 +96,7 @@
 ):
     states = history.shape[0]
     stacked = jnp.concatenate([history, cotangent[None]], axis=0)
-    arrived = lax.all_to_all(stacked, "seq", split_axis=2, concat_axis=1, tiled=True)
+    arrived = swapped_with_each(stacked, "seq", 2, 1)
     arrived_rows = jnp.swapaxes(arrived, 1, 2)
     hist_local = arrived_rows[:states]
     cot_local = arrived_rows[states]

time: 712 us -> 709 us (level)
    all_to_all x1 -> x0, waiting for transfers between devices: 64.4 us -> none  [per_device(): lax.all_to_all(stacked, 'seq', split_axis=2, concat_axis=1, tiled=True)]
    all_gather x1, waiting for transfers between devices: 33.5 us -> 70 us  [per_device(): piece = lax.all_gather(w_in, 'seq', axis=0, tiled=True)]
    ppermute x0 -> x7, waiting for transfers between devices: none -> 20.8 us  [swapped_with_each(): part = lax.ppermute(part, axis, [(d, d ^ mask) for d in range(ways)])]
    all_to_all x2 -> x0, local copies, waits for them, and re-layouts: 9.41 us -> none  [per_device(): lax.all_to_all(stacked, 'seq', split_axis=2, concat_axis=1, tiled=True)]
    dynamic_update_slice x0 -> x7, local copies, waits for them, and re-layouts: none -> 9.35 us  [swapped_with_each(): lax.dynamic_update_slice_in_dim(full, part, (here ^ mask) * height, axis=...]
    ppermute x0 -> x7, starting transfers between devices: none -> 7.38 us  [swapped_with_each(): part = lax.ppermute(part, axis, [(d, d ^ mask) for d in range(ways)])]
    unnamed x218 -> x217, local copies, waits for them, and re-layouts: 50.6 us -> 48 us
  transfers between devices with their start and end apart: 9 -> 15, of which waited for: 5 -> 8; matrix products, arithmetic and copies ran while one was open for 36% -> 37% of each run, Pallas kernels for 0% -> 0%
where the time goes in v1:
time: 709 us; the launch traced here: 698 us
  waiting for transfers between devices  282 us (40%)
  matrix products  149 us (21%)
  local copies, waits for them, and re-layouts  113 us (16%)
  blocking collectives  81.4 us (11%)
  other arithmetic  43.4 us (6%)
  between operations  15.9 us (2%)
  starting transfers between devices  12.7 us (2%)
    psum x1, waiting for transfers between devices, per_device(): lax.psum((gen_gain_grad, gen_in_grad, gen_out_grad, gen_bias_grad, norm_g...  121 us
    psum x1, blocking collectives, per_device(): lax.psum((gen_gain_grad, gen_in_grad, gen_out_grad, gen_bias_grad, norm_g...  81.4 us
    all_gather x1, waiting for transfers between devices, per_device(): piece = lax.all_gather(w_in, 'seq', axis=0, tiled=True)  70 us
    reduce_scatter x1, waiting for transfers between devices, per_device(): lax.psum_scatter(jnp.concatenate([term_out, term_down], axis=1).astype(jn...  51.6 us
    unnamed x217, local copies, waits for them, and re-layouts  48 us
    dot_general x9, matrix products, per_device(): jnp.einsum('std,td->ts', grad_streams, hist_local[state].astype(jnp.float...  44.5 us
    dot_general x9, matrix products, per_device(): jnp.einsum('ts,std->td', mixing[:, :, state], grad_streams, precision=hig...  40.6 us
    ppermute x7, waiting for transfers between devices, swapped_with_each(): part = lax.ppermute(part, axis, [(d, d ^ mask) for d in range(ways)])  20.8 us
  transfers between devices with their start and end apart: 15, of which 8 were waited for; matrix products, arithmetic and copies ran while one was open for 37% of the time, Pallas kernels for 0%

profile of v1, /device:TPU:8, one launch (start us, length us, event | category | flops | bytes accessed | tf_op | source)
XLA Modules:
  0.0 697.6 jit_solution(7457640394124598077)
XLA Ops:
  33.2 6.4 collective-permute-done.2
  44.0 6.8 collective-permute-done.5
  51.5 5.2 collective-permute-done.6
  72.2 70.0 %all-gather.4.cloned.1.call-done = bf16[1024,7,1024]{2,0,1:T(8,128)(2,1)} async-done(((bf16[128,7,1024]{2,0,1:T(8,128)(2,1)}), bf16[1024,7,1024]{2,0,1:T(8,128)(2,1)}) %all-gather.4.cloned.1.call-update) | async-done | bytes 14680080 | tf_op jit(solution)/shard_map/all_gather | solution.py:123
  142.2 5.0 fusion.6
  147.2 6.3 fusion.22
  176.1 6.9 multiply_convert_fusion
  182.9 17.0 %all-gather.8.cloned.1.call-done = bf16[1024,4096]{0,1:T(8,128)(2,1)} async-done(((bf16[128,4096]{0,1:T(8,128)(2,1)}), bf16[1024,4096]{0,1:T(8,128)(2,1)}) %all-gather.8.cloned.1.call-update) | async-done | bytes 8388624 | tf_op jit(solution)/shard_map/all_gather | solution.py:154
  200.0 8.0 %fusion.15 = f32[4,128,1024]{2,1,0:T(8,128)S(1)} fusion(f32[4,128,1024]{2,1,0:T(8,128)} %get-tuple-element.91, f32[7,128,1024]{2,1,0:T(8,128)} %copy-done.2, bf16[1024,4,1024]{0,2,1:T(8,128)(2,1)} %bitcast.354, pred[128]{0:T(512)(128)(4,1)S(1)} %copy-done.56, bf16[10,128,1024]{2,1,0:T(8,128)(2,1)} %bitcast.1), kind=kOutput, calls=%fused_computation.34 | convolution fusion | flops 1080688640 | bytes 14942336 | tf_op jit(solution)/shard_map/tn,njk->jtk/dot_general | solution.py:166
  214.2 8.3 %pad_maximum_fusion = bf16[1024,7,1024]{0,2,1:T(8,128)(2,1)} fusion(bf16[1024,4,1024]{0,2,1:T(8,128)(2,1)S(1)} %convert_bitcast_fusion, bf16[1024,3,1024]{0,2,1:T(8,128)(2,1)S(1)} %convert_bitcast_fusion.1), kind=kLoop, calls=%fused_computation | loop fusion | flops 7340032 | bytes 29360128 | tf_op jit(solution)/shard_map/concatenate | solution.py:225
  222.5 20.0 %copy.159 = bf16[1024,7168]{1,0:T(8,128)(2,1)} copy(bf16[1024,7168]{0,1:T(8,128)(2,1)} %bitcast.352) | data formatting | bytes 29360128
  257.0 6.3 pad_maximum_fusion.1
  270.6 5.9 multiply_reduce_fusion.5
  276.5 5.0 multiply_reduce_fusion.1
  284.0 4.8 fusion.68
  288.8 4.8 fusion.66
  293.7 5.0 fusion.64
  298.8 4.8 fusion.62
  304.2 4.8 fusion.60
  309.7 5.2 fusion.58
  315.6 4.8 fusion.56
  321.0 4.8 fusion.54
  326.5 5.6 fusion.52
  336.1 5.2 fusion.163
  341.3 4.9 convolution_bitcast_fusion.1
  365.3 4.6 fusion.155
  381.1 51.6 %reduce-scatter.5.cloned.1.call-done = bf16[128,5120]{1,0:T(8,128)(2,1)} async-done(((bf16[1024,5120]{1,0:T(8,128)(2,1)}), bf16[128,5120]{1,0:T(8,128)(2,1)}) %reduce-scatter.5.cloned.1.call-update) | async-done | bytes 1310736 | tf_op jit(solution)/shard_map/reduce_scatter | solution.py:175
  443.1 4.6 fusion.147
  449.7 6.8 copy.102
  456.6 4.9 all-to-all-start
  465.2 81.4 %all-reduce = (f32[4,9]{1,0:T(4,128)S(1)}, f32[]{:T(128)}, f32[4,9]{1,0:T(4,128)S(1)}, f32[1024]{0:T(1024)}, f32[40,4,9]{0,2,1:T(8,128)S(1)}, /*index=5*/f32[4,9...) all-reduce(f32[4,9]{1,0:T(4,128)S(1)} %copy-done.84, ...), channel_id=1, replica_groups=mesh['seq'=8,'dp'=4] {'seq','dp'}, use_global_device_ids=true, to_apply=%region_12.13 | all-reduce | flops 14861 | bytes 118888 | tf_op jit(solution)/shard_map/psum | solution.py:276
  567.2 121.5 %all-reduce.5.cloned.1.call-done = f32[1024,40]{0,1:T(8,128)} async-done(((f32[1024,40]{0,1:T(8,128)}), f32[1024,40]{0,1:T(8,128)}) %all-reduce.5.cloned.1.call-update) | async-done | bytes 163856 | tf_op jit(solution)/shard_map/psum | solution.py:276
  (362 shorter events, 174.9 us)
Async XLA Ops:
  7.2 52.7 %copy-start = (bf16[1024,40]{0,1:T(8,128)(2,1)S(1)}, bf16[1024,40]{0,1:T(8,128)(2,1)}, u32[]{:S(2)}) copy-start(bf16[1024,40]{0,1:T(8,128)(2,1)} %param.20) | copy-start | bytes 245764
  7.2 62.3 %all-gather.6.cloned.1.call-start = ((), (), s32[]{:S(2)}) async-start(), calls=%async_computation.4 | async-start | bytes 2359296 | tf_op jit(solution)/shard_map/all_gather | solution.py:154
  7.9 134.2 %all-gather.4.cloned.1.call-start = ((), (), s32[]{:S(2)}) async-start(), calls=%async_computation.3 | async-start | bytes 16515072 | tf_op jit(solution)/shard_map/all_gather | solution.py:123
  8.7 191.3 %all-gather.8.cloned.1.call-start = ((), (), s32[]{:S(2)}) async-start(), calls=%async_computation.5 | async-start | bytes 9437184 | tf_op jit(solution)/shard_map/all_gather | solution.py:154
  10.1 367.1 %reduce-scatter.7.cloned.1.call-start = ((), (), s32[]{:S(2)}) async-start(), calls=%async_computation.8 | async-start | bytes 16515072
  16.4 7.3 %collective-permute-start = (bf16[10,128,128]{1,2,0:T(8,128)(2,1)}, bf16[10,128,128]{1,2,0:T(8,128)(2,1)}, u32[]{:S(2)}, u32[]{:S(2)}) collective-permute-start(bf16[10,128,128]{1,2,0:T(8,128)(2,1)} %get-tuple-element.116), channel_id=1, source_target_pairs={{0,4},{4,0},{8,12},{12,8},{16,20},{20,16},{24,28},{28,24},{1,5},{5... | collective-permute-start | bytes 983048 | tf_op jit(solution)/shard_map/ppermute | solution.py:27
  16.5 13.8 %collective-permute-start.1 = (bf16[10,128,128]{1,2,0:T(8,128)(2,1)}, bf16[10,128,128]{1,2,0:T(8,128)(2,1)}, u32[]{:S(2)}, u32[]{:S(2)}) collective-permute-start(bf16[10,128,128]{1,2,0:T(8,128)(2,1)} %get-tuple-element.117), channel_id=1, source_target_pairs={{0,8},{4,12},{8,0},{12,4},{16,24},{20,28},{24,16},{28,20},{1,9},{5... | collective-permute-start | bytes 983048 | tf_op jit(solution)/shard_map/ppermute | solution.py:27
  18.0 21.6 %collective-permute-start.2 = (bf16[10,128,128]{1,2,0:T(8,128)(2,1)}, bf16[10,128,128]{1,2,0:T(8,128)(2,1)}, u32[]{:S(2)}, u32[]{:S(2)}) collective-permute-start(bf16[10,128,128]{1,2,0:T(8,128)(2,1)} %get-tuple-element.118), channel_id=1, source_target_pairs={{0,12},{4,8},{8,4},{12,0},{16,28},{20,24},{24,20},{28,16},{1,13},{... | collective-permute-start | bytes 983048 | tf_op jit(solution)/shard_map/ppermute | solution.py:27
  18.3 23.1 %collective-permute-start.3 = (bf16[10,128,128]{1,2,0:T(8,128)(2,1)S(1)}, bf16[10,128,128]{1,2,0:T(8,128)(2,1)}, u32[]{:S(2)}, u32[]{:S(2)}) collective-permute-start(bf16[10,128,128]{1,2,0:T(8,128)(2,1)S(1)} %get-tuple-element.119), channel_id=1, source_target_pairs={{0,16},{4,20},{8,24},{12,28},{16,0},{20,4},{24,8},{28,12},{1,17},{... | collective-permute-start | bytes 983048 | tf_op jit(solution)/shard_map/ppermute | solution.py:27
  19.9 23.3 %collective-permute-start.4 = (bf16[10,128,128]{1,2,0:T(8,128)(2,1)S(1)}, bf16[10,128,128]{1,2,0:T(8,128)(2,1)S(1)}, u32[]{:S(2)}, u32[]{:S(2)}) collective-permute-start(bf16[10,128,128]{1,2,0:T(8,128)(2,1)S(1)} %get-tuple-element.121), channel_id=1, source_target_pairs={{0,20},{4,16},{8,28},{12,24},{16,4},{20,0},{24,12},{28,8},{1,21},{... | collective-permute-start | bytes 983048 | tf_op jit(solution)/shard_map/ppermute | solution.py:27
  22.7 46.8 %copy-start.55 = (pred[128]{0:T(512)(128)(4,1)}, pred[128]{0:T(512)(128)(4,1)S(1)}, u32[]{:S(2)}) copy-start(pred[128]{0:T(512)(128)(4,1)S(1)} %get-tuple-element.89) | copy-start | bytes 388
  22.8 119.4 %copy-start.77 = (f32[1,1024]{1,0:T(1,128)}, f32[1,1024]{1,0:T(1,128)S(1)}, u32[]{:S(2)}) copy-start(f32[1,1024]{1,0:T(1,128)S(1)} %get-tuple-element.145) | copy-start | bytes 12292
  22.8 124.4 %copy-start.81 = (f32[1,1024]{1,0:T(1,128)}, f32[1,1024]{1,0:T(1,128)S(1)}, u32[]{:S(2)}) copy-start(f32[1,1024]{1,0:T(1,128)S(1)} %get-tuple-element.146) | copy-start | bytes 12292
  23.7 27.1 %collective-permute-start.5 = (bf16[10,128,128]{1,2,0:T(8,128)(2,1)S(1)}, bf16[10,128,128]{1,2,0:T(8,128)(2,1)S(1)}, u32[]{:S(2)}, u32[]{:S(2)}) collective-permute-start(bf16[10,128,128]{1,2,0:T(8,128)(2,1)S(1)} %get-tuple-element.120), channel_id=1, source_target_pairs={{0,24},{4,28},{8,16},{12,20},{16,8},{20,12},{24,0},{28,4},{1,25},{... | collective-permute-start | bytes 983048 | tf_op jit(solution)/shard_map/ppermute | solution.py:27
  30.3 29.6 %copy-start.87 = (f32[1024]{0:T(1024)S(1)}, f32[1024]{0:T(1024)}, u32[]{:S(2)}) copy-start(f32[1024]{0:T(1024)} %param.19) | copy-start | bytes 12292
  30.3 26.5 %collective-permute-start.6 = (bf16[10,128,128]{1,2,0:T(8,128)(2,1)S(1)}, bf16[10,128,128]{1,2,0:T(8,128)(2,1)S(1)}, u32[]{:S(2)}, u32[]{:S(2)}) collective-permute-start(bf16[10,128,128]{1,2,0:T(8,128)(2,1)S(1)} %get-tuple-element.114), channel_id=1, source_target_pairs={{0,28},{4,24},{8,20},{12,16},{16,12},{20,8},{24,4},{28,0},{1,29},{... | collective-permute-start | bytes 983048 | tf_op jit(solution)/shard_map/ppermute | solution.py:27
  41.4 19.8 %copy-start.43 = (f32[40,4,9]{0,1,2:T(4,128)S(1)}, f32[40,4,9]{0,1,2:T(4,128)}, u32[]{:S(2)}) copy-start(f32[40,4,9]{0,1,2:T(4,128)} %param.21) | copy-start | bytes 17284
  41.4 19.8 %copy-start.94 = (f32[4,9]{1,0:T(4,128)S(1)}, f32[4,9]{1,0:T(4,128)}, u32[]{:S(2)}) copy-start(f32[4,9]{1,0:T(4,128)} %param.22) | copy-start | bytes 436
  176.1 23.9 %copy-start.56 = (pred[128]{0:T(512)(128)(4,1)S(1)}, pred[128]{0:T(512)(128)(4,1)}, u32[]{:S(2)}) copy-start(pred[128]{0:T(512)(128)(4,1)} %copy-done.55) | copy-start | bytes 388
  200.0 9.3 %copy-start.10 = (f32[1,128,1024]{2,1,0:T(8,128)S(1)}, f32[1,128,1024]{2,1,0:T(8,128)}, u32[]{:S(2)}) copy-start(f32[1,128,1024]{2,1,0:T(8,128)} %copy.100) | copy-start | bytes 1572868
  200.0 9.3 %copy-start.12 = (f32[1,128,1024]{2,1,0:T(8,128)S(1)}, f32[1,128,1024]{2,1,0:T(8,128)}, u32[]{:S(2)}) copy-start(f32[1,128,1024]{2,1,0:T(8,128)} %copy.99) | copy-start | bytes 1572868
  200.0 9.3 %copy-start.14 = (f32[1,128,1024]{2,1,0:T(8,128)S(1)}, f32[1,128,1024]{2,1,0:T(8,128)}, u32[]{:S(2)}) copy-start(f32[1,128,1024]{2,1,0:T(8,128)} %copy.98) | copy-start | bytes 1572868
  242.6 190.1 %reduce-scatter.5.cloned.1.call-start = ((), (), s32[]{:S(2)}) async-start(), calls=%async_computation.7 | async-start | bytes 11796480 | tf_op jit(solution)/shard_map/reduce_scatter | solution.py:175
  263.4 7.3 %copy-start.58 = (f32[4,128]{1,0:T(4,128)S(1)}, f32[4,128]{1,0:T(4,128)}, u32[]{:S(2)}) copy-start(f32[4,128]{1,0:T(4,128)} %copy-done.57) | copy-start | bytes 6148
  263.4 296.3 %all-reduce.7.cloned.1.call-start = ((), (), s32[]{:S(2)}) async-start(), calls=%async_computation.9 | async-start | bytes 6291456 | tf_op jit(solution)/shard_map/psum | solution.py:271
  332.0 9.3 %copy-start.3 = (bf16[4,128,1024]{2,1,0:T(8,128)(2,1)S(1)}, bf16[4,128,1024]{2,1,0:T(8,128)(2,1)}, u32[]{:S(2)}) copy-start(bf16[4,128,1024]{2,1,0:T(8,128)(2,1)} %get-tuple-element.90) | copy-start | bytes 3145732
  381.1 51.6 %copy-start.37 = (f32[128,4,1]{1,2,0:T(1,128)S(1)}, f32[128,4,1]{1,2,0:T(1,128)}, u32[]{:S(2)}) copy-start(f32[128,4,1]{1,2,0:T(1,128)} %copy.130) | copy-start | bytes 6148
  456.5 7.0 %copy-start.6 = (f32[4,128,1024]{2,1,0:T(8,128)S(1)}, f32[4,128,1024]{2,1,0:T(8,128)}, u32[]{:S(2)}) copy-start(f32[4,128,1024]{2,1,0:T(8,128)} %copy-done.5) | copy-start | bytes 6291460
  456.5 7.0 %copy-start.11 = (f32[1,128,1024]{2,1,0:T(8,128)S(1)}, f32[1,128,1024]{2,1,0:T(8,128)}, u32[]{:S(2)}) copy-start(f32[1,128,1024]{2,1,0:T(8,128)} %copy.100) | copy-start | bytes 1572868
  456.5 7.0 %copy-start.13 = (f32[1,128,1024]{2,1,0:T(8,128)S(1)}, f32[1,128,1024]{2,1,0:T(8,128)}, u32[]{:S(2)}) copy-start(f32[1,128,1024]{2,1,0:T(8,128)} %copy.99) | copy-start | bytes 1572868
  456.6 91.9 %all-to-all-start = ((bf16[10,1024,128]{2,0,1:T(8,128)(2,1)}), bf16[10,1024,128]{2,0,1:T(8,128)(2,1)}, u32[]{:S(2)}, u32[]{:S(2)}) async-start(bf16[10,1024,128]{2,0,1:T(8,128)(2,1)} %copy.102), calls=%async_computation | async-start | bytes 8388608 | tf_op jit(solution)/shard_map/all_to_all | solution.py:269
  461.4 227.3 %all-reduce.5.cloned.1.call-start = ((), (), s32[]{:S(2)}) async-start(), calls=%async_computation.6 | async-start | bytes 327680 | tf_op jit(solution)/shard_map/psum | solution.py:276
  (83 other events, 307.3 us)
Sparse Core Ops, SparseCore 0:
  9.9 49.4 all-gather.5
  61.3 80.8 all-gather.3
  144.1 55.8 all-gather.7
  242.7 104.6 reduce-scatter.6
  350.7 81.9 reduce-scatter.4
  435.0 120.2 all-reduce.6
  561.4 127.2 all-reduce.4
